TPU v7x, 32 devices: a whole 2x2x4 slice. The times are simulated.
32 devices in a mesh: cohort: 2 (over x), region: 16 (over z, y, core).
Axes of the slice: x: 2, y: 2, z: 4, core: 2. Of those that a mesh axis runs over, the one named last changes fastest.
Arguments:
- dosage: bfloat16 [4096, 16384], P('cohort', 'region'), parts along dimension 0, may hold values from 0 to 2, as said below
- eigvec: bfloat16 [16384, 2048], P('region', 'cohort'), parts along dimension 1, may hold values from -1 to 1, as said below
- eigval: float32 [2, 16384], P('cohort', 'region'), parts along dimension 0, may hold values from 64 to 65536
- pheno: bfloat16 [4096, 128], P('cohort'), parts along dimension 0, may hold values from 0 to 1, as said below
Outputs:
- level1_weights: float32 [128, 128], P('region', 'cohort'), parts along dimension 1
There are 2 independent parts, one for each index of `cohort`. A program takes and returns all parts, laid end to end along the dimension named above; each array names one. Nothing has to cross between parts.
Inputs may be any that keep to these rules, and one draw needn't show every extreme that they name: Every entry is a whole dosage 0, 1 or 2. `eigvec`: the rows of each block form an orthonormal basis up to rounding. `pheno`: every entry is 0 or 1.
All inputs are finite; a program needn't handle non-finite values.
Results may differ from a plain program's by a relative error of at most 0.0051.
Values may be sent and summed in bfloat16 or wider, within the bound.
No kernel may reach another device: no remote copies, remote signals or barrier semaphores. Data moves between devices by JAX's collectives and lax.ppermute only.
A program may use at most 64 MiB of HBM per device.

v0:
```python
import jax
import jax.numpy as jnp
from jax import lax
from jax.sharding import PartitionSpec as P

NEWTON = 3
EPSILON = 1e-05
HERITABILITY = (0.01, 0.25, 0.75, 0.99)
LEVEL_ONE = 0.03125


def standardize(values):
    values = values.astype(jnp.float32)
    center = jnp.mean(values, axis=0)
    spread = jnp.sqrt(jnp.mean(jnp.square(values - center), axis=0) + EPSILON)
    return ((values - center) / spread).astype(jnp.bfloat16)


def fit_traits(moved, target, total_samples):
    count_traits = moved.shape[1]
    design = jnp.moveaxis(moved, 1, 0).reshape(count_traits, -1, moved.shape[3])
    predictors = design.shape[1]
    level_ridge = LEVEL_ONE * total_samples
    all_weights = jnp.zeros((count_traits, predictors), jnp.float32)
    own_weights = jnp.zeros((count_traits, predictors), jnp.float32)
    identity = jnp.eye(predictors, dtype=jnp.float32)
    for newton_step in range(NEWTON):
        logits = jnp.einsum(
            "kqn,kq->kn",
            design,
            all_weights.astype(jnp.bfloat16),
            preferred_element_type=jnp.float32,
        )
        prob = jax.nn.sigmoid(logits)
        resid = (target - prob).astype(jnp.bfloat16)
        weighted = (design * (prob * (1.0 - prob))[:, None, :]).astype(jnp.bfloat16)
        gram = jnp.einsum("kqn,kpn->kqp", weighted, design, preferred_element_type=jnp.float32)
        grad = jnp.einsum("kqn,kn->kq", design, resid, preferred_element_type=jnp.float32)
        grad = grad - level_ridge * own_weights
        factor = jnp.linalg.cholesky(gram + level_ridge * identity)
        partial_solve = lax.linalg.triangular_solve(
            factor, grad[:, :, None], left_side=True, lower=True
        )
        update = lax.linalg.triangular_solve(
            factor, partial_solve, left_side=True, lower=True, transpose_a=True
        )
        own_weights = own_weights + update[:, :, 0]
        all_weights = own_weights
    return own_weights


def on_device(dosage, eigvec, eigval, pheno):
    samples, width = dosage.shape
    traits = pheno.shape[1]
    regions = lax.axis_size("region")
    ridges = len(HERITABILITY)
    per_device = traits // regions
    shrink = jnp.array([width * (1.0 - value) / value for value in HERITABILITY], jnp.float32)
    std_trait = standardize(pheno)
    std_geno = standardize(dosage)
    cross = lax.dot_general(
        std_geno, std_trait, (((0,), (0,)), ((), ())), preferred_element_type=jnp.float32
    ).astype(jnp.bfloat16)
    rotated = lax.dot_general(
        eigvec, cross, (((0,), (0,)), ((), ())), preferred_element_type=jnp.float32
    )
    scaled = (rotated[:, None, :] / (eigval[0][:, None, None] + shrink[None, :, None])).astype(
        jnp.bfloat16
    )
    ridge = jnp.dot(
        eigvec, scaled.reshape(width, ridges * traits), preferred_element_type=jnp.float32
    ).astype(jnp.bfloat16)
    position = lax.axis_index("region")
    predicted = lax.dot_general(
        ridge, std_geno, (((0,), (1,)), ((), ())), preferred_element_type=jnp.float32
    ).astype(jnp.bfloat16)
    predicted = predicted.reshape(ridges, traits, 1, samples)
    moved = lax.all_to_all(predicted, "region", split_axis=1, concat_axis=2, tiled=True)
    target = lax.dynamic_slice_in_dim(pheno, position * per_device, per_device, 1)
    weights = fit_traits(moved, target.astype(jnp.float32).T, samples)
    return weights


def solution(mesh):
    return jax.shard_map(
        on_device,
        mesh=mesh,
        in_specs=(
            P("cohort", "region"),
            P("region", "cohort"),
            P("cohort", "region"),
            P("cohort", None),
        ),
        out_specs=P("region", "cohort"),
        check_vma=False,
    )
```

profile of v0, /device:TPU:13, one launch (start us, length us, event | category | flops | bytes accessed | tf_op | source)
XLA Modules:
  0.0 363.7 jit_solution(3730043652886165444)
XLA Ops:
  0.0 3.0 convert_reduce_fusion
  3.1 0.5 copy-done.1
  3.6 1.1 fusion.2
  4.8 3.2 fusion.3
  8.0 0.3 convert_reduce_fusion.1
  8.3 0.3 fusion.27
  8.6 5.0 %convolution_bitcast_fusion = f32[1024,128]{0,1:T(8,128)} fusion(bf16[1024,1024]{1,0:T(8,128)(2,1)S(1)} %copy-done, bf16[2048,1024]{1,0:T(8,128)(2,1)} %fusion.3, bf16[2048,128]{1,0:T(8,128)(2,1)S(1)} %copy-done.5, f32[128]{0:T(128)S(1)} %add_sqrt_fusion.1, f32[128]{0:T(128)S(1)} %broadcast_multiply_fusion.1), kind=kOutput, calls=%fused_computation.25 | convolution fusion | flops 806486016 | bytes 7341056 | tf_op jit(solution)/shard_map/dot_general | solution.py:64
  13.6 1.2 copy.50
  14.9 0.2 broadcast_add_fusion
  15.1 4.6 %divide_convert_fusion = bf16[1024,4,128]{2,1,0:T(4,128)(2,1)} fusion(f32[1024,4]{1,0:T(8,128)S(1)} %broadcast_add_fusion, f32[1024,128]{1,0:T(8,128)S(1)} %copy.50), kind=kLoop, calls=%fused_computation.16 | loop fusion | flops 1048576 | bytes 1589248 | tf_op jit(solution)/shard_map/convert_element_type | solution.py:67
  19.7 7.3 %convolution_convert_fusion = bf16[512,2048]{1,0:T(8,128)(2,1)} fusion(bf16[2048,1024]{1,0:T(8,128)(2,1)} %fusion.3, bf16[1024,1024]{1,0:T(8,128)(2,1)S(1)} %copy-done, bf16[128,8,4,128]{3,2,1,0:T(4,128)(2,1)} %bitcast.211), kind=kOutput, calls=%fused_computation.15 | convolution fusion | flops 3222798336 | bytes 9437184 | tf_op jit(solution)/shard_map/dot_general | solution.py:74
  27.0 4.6 %copy.51 = bf16[4,128,1,2048]{3,0,2,1:T(4,128)(2,1)} copy(bf16[4,128,1,2048]{3,1,0,2:T(8,128)(2,1)} %bitcast.210) | data formatting | bytes 4194304 | tf_op jit(solution)/shard_map/reshape | solution.py:77
  31.6 6.7 %all-to-all-start = ((bf16[4,128,1,2048]{3,0,2,1:T(4,128)(2,1)}), bf16[4,128,1,2048]{3,0,2,1:T(4,128)(2,1)}, u32[]{:S(2)}, u32[]{:S(2)}) async-start(bf16[4,128,1,2048]{3,0,2,1:T(4,128)(2,1)} %copy.51), calls=%async_computation | async-start | bytes 4194304 | tf_op jit(solution)/shard_map/all_to_all | solution.py:78
  38.3 0.2 constant_dynamic-slice_fusion
  38.5 0.2 copy.90
  38.7 47.1 %all-to-all-done = bf16[4,128,1,2048]{3,0,2,1:T(4,128)(2,1)} async-done(((bf16[4,128,1,2048]{3,0,2,1:T(4,128)(2,1)}), bf16[4,128,1,2048]{3,0,2,1:T(4,128)(2,1)}, u32[]{:S(2)}, u32[]{:S(2)}) %all-to-all-start) | async-done | bytes 2097184 | tf_op jit(solution)/shard_map/all_to_all | solution.py:78
  85.8 2.8 copy.52
  88.6 0.4 fusion.76
  89.0 0.9 copy-done.2
  89.9 0.7 fusion.18
  90.7 0.1 copy.54
  90.9 46.9 %custom-call.15 = f32[8,64,64]{2,1,0:T(8,128)S(1)} custom-call(f32[8,64,64]{2,1,0:T(8,128)S(1)} %fusion.50), custom_call_target="Cholesky" | custom-call | tf_op jit(solution)/shard_map/jit(cholesky)/cholesky | solution.py:40
  137.8 0.1 compare_reduce_fusion.2
  137.9 0.1 select_bitcast_fusion.2
  138.1 39.3 %custom-call.17 = f32[8,1,64,64]{2,3,1,0:T(8,128)S(1)} custom-call(f32[8,1,64,64]{3,2,1,0:T(8,128)S(1)} %select_bitcast_fusion.2), custom_call_target="InvertDiagBlocksLowerTriangular" | custom-call | tf_op jit(solution)/shard_map/triangular_solve/custom-call.2 | solution.py:44
  177.4 2.4 convolution_bitcast_fusion.4
  179.8 0.4 convolution_bitcast_fusion.3
  180.1 0.5 fusion.48
  180.7 0.4 fusion.74
  181.1 0.8 fusion.21
  181.9 0.1 copy.58
  182.1 46.9 %custom-call.18 = f32[8,64,64]{2,1,0:T(8,128)S(1)} custom-call(f32[8,64,64]{2,1,0:T(8,128)S(1)} %fusion.46), custom_call_target="Cholesky" | custom-call | tf_op jit(solution)/shard_map/jit(cholesky)/cholesky | solution.py:40
  229.0 0.1 compare_reduce_fusion.1
  229.1 0.1 select_bitcast_fusion.1
  229.2 39.3 %custom-call.20 = f32[8,1,64,64]{2,3,1,0:T(8,128)S(1)} custom-call(f32[8,1,64,64]{3,2,1,0:T(8,128)S(1)} %select_bitcast_fusion.1), custom_call_target="InvertDiagBlocksLowerTriangular" | custom-call | tf_op jit(solution)/shard_map/triangular_solve/custom-call.2 | solution.py:44
  268.6 2.4 fusion.65
  271.0 0.4 convolution_bitcast_fusion.2
  271.3 0.5 fusion.44
  271.9 0.4 fusion.72
  272.3 0.7 fusion.24
  273.0 0.1 copy.61
  273.2 47.1 %custom-call.21 = f32[8,64,64]{2,1,0:T(8,128)S(1)} custom-call(f32[8,64,64]{2,1,0:T(8,128)S(1)} %fusion.42), custom_call_target="Cholesky" | custom-call | tf_op jit(solution)/shard_map/jit(cholesky)/cholesky | solution.py:40
  320.4 0.1 compare_reduce_fusion
  320.6 39.3 %custom-call.23 = f32[8,1,64,64]{2,3,1,0:T(8,128)S(1)} custom-call(f32[8,1,64,64]{3,2,1,0:T(8,128)S(1)} %select_bitcast_fusion), custom_call_target="InvertDiagBlocksLowerTriangular" | custom-call | tf_op jit(solution)/shard_map/triangular_solve/custom-call.2 | solution.py:44
  359.9 2.2 fusion.63
  362.2 0.4 convolution_bitcast_fusion.1
  362.5 0.5 fusion.40
  363.1 0.6 add_bitcast_fusion
  (35 shorter events, 0.6 us)
Async XLA Ops:
  0.0 8.6 %copy-start = (bf16[1024,1024]{1,0:T(8,128)(2,1)S(1)}, bf16[1024,1024]{1,0:T(8,128)(2,1)}, u32[]{:S(2)}) copy-start(bf16[1024,1024]{1,0:T(8,128)(2,1)} %param.11) | copy-start | bytes 6291460
  0.0 3.6 copy-start.1
  4.8 3.2 copy-start.5
  8.6 6.3 %copy-start.6 = (f32[1,1024]{1,0:T(1,128)S(1)}, f32[1,1024]{1,0:T(1,128)}, u32[]{:S(2)}) copy-start(f32[1,1024]{1,0:T(1,128)} %param.12) | copy-start | bytes 12292
  8.6 6.3 %copy-start.7 = (f32[4]{0:T(128)S(1)}, f32[4]{0:T(128)}, u32[]{:S(2)}) copy-start(f32[4]{0:T(128)} %constant.65.clone) | copy-start | bytes 52
  31.6 54.3 %all-to-all-start = ((bf16[4,128,1,2048]{3,0,2,1:T(4,128)(2,1)}), bf16[4,128,1,2048]{3,0,2,1:T(4,128)(2,1)}, u32[]{:S(2)}, u32[]{:S(2)}) async-start(bf16[4,128,1,2048]{3,0,2,1:T(4,128)(2,1)} %copy.51), calls=%async_computation | async-start | bytes 4194304 | tf_op jit(solution)/shard_map/all_to_all | solution.py:78
  88.6 1.4 copy-start.2
  177.4 3.3 copy-start.3
  268.6 3.3 copy-start.4
where the time goes:
time: 364 us
  other arithmetic  273 us (75%)
  waiting for transfers between devices  47.1 us (13%)
  matrix products  25.4 us (7%)
  local copies, waits for them, and re-layouts  10.8 us (3%)
  starting transfers between devices  6.74 us (2%)
    another operation x10, other arithmetic, fit_traits(): factor = jnp.linalg.cholesky(gram + level_ridge * identity)  141 us
    another operation x7, other arithmetic, fit_traits(): lax.linalg.triangular_solve(factor, partial_solve, left_side=True, lower=...  118 us
    all_to_all x1, waiting for transfers between devices, on_device(): lax.all_to_all(predicted, 'region', split_axis=1, concat_axis=2, tiled=True)  47.1 us
    dot_general x1, matrix products, on_device(): lax.dot_general(ridge, std_geno, (((0,), (1,)), ((), ())), preferred_elem...  7.31 us
  transfers between devices with their start and end apart: 1, of which 1 were waited for; matrix products, arithmetic and copies ran while one was open for 0% of the time, Pallas kernels for 0%

commit v1 on v0

--- a/solution.py
+++ b/solution.py
@@ -7,6 +7,13 @@
 EPSILON = 1e-05
 HERITABILITY = (0.01, 0.25, 0.75, 0.99)
 LEVEL_ONE = 0.03125
+
+
+def trade_parts(x, axis, split, join):
+    count = lax.axis_size(axis)
+    blocks = jnp.stack(jnp.split(x, count, axis=split), axis=0)
+    blocks = lax.all_to_all(blocks, axis, split_axis=0, concat_axis=0)
+    return jnp.concatenate(blocks, axis=join)
 
 
 def standardize(values):
@@ -75,7 +82,7 @@
         ridge, std_geno, (((0,), (1,)), ((), ())), preferred_element_type=jnp.float32
     ).astype(jnp.bfloat16)
     predicted = predicted.reshape(ridges, traits, 1, samples)
-    moved = lax.all_to_all(predicted, "region", split_axis=1, concat_axis=2, tiled=True)
+    moved = trade_parts(predicted, "region", 1, 2)
     target = lax.dynamic_slice_in_dim(pheno, position * per_device, per_device, 1)
     weights = fit_traits(moved, target.astype(jnp.float32).T, samples)
     return weights

time: 364 us -> 377 us (1.036)
  local copies, waits for them, and re-layouts: 10.8 us -> 24.1 us
    unnamed x17 -> x34, local copies, waits for them, and re-layouts: 1.67 us -> 18.9 us
    reshape x1 -> x0, local copies, waits for them, and re-layouts: 4.56 us -> none  [on_device(): predicted = predicted.reshape(ridges, traits, 1, samples)]
where the time goes in v1:
time: 377 us
  other arithmetic  273 us (72%)
  waiting for transfers between devices  47.1 us (12%)
  matrix products  25.4 us (7%)
  local copies, waits for them, and re-layouts  24.1 us (6%)
  starting transfers between devices  6.56 us (2%)
    another operation x10, other arithmetic, fit_traits(): factor = jnp.linalg.cholesky(gram + level_ridge * identity)  141 us
    another operation x7, other arithmetic, fit_traits(): lax.linalg.triangular_solve(factor, partial_solve, left_side=True, lower=...  118 us
    all_to_all x1, waiting for transfers between devices, trade_parts(): blocks = lax.all_to_all(blocks, axis, split_axis=0, concat_axis=0)  47.1 us
    unnamed x34, local copies, waits for them, and re-layouts  18.9 us
  transfers between devices with their start and end apart: 1, of which 1 were waited for; matrix products, arithmetic and copies ran while one was open for 0% of the time, Pallas kernels for 0%

profile of v1, /device:TPU:13, one launch (start us, length us, event | category | flops | bytes accessed | tf_op | source)
XLA Modules:
  0.0 376.8 jit_solution(39605860104783510)
XLA Ops:
  0.0 3.0 convert_reduce_fusion
  3.1 0.5 copy-done.1
  3.6 1.1 fusion.2
  4.8 3.2 fusion.3
  8.6 5.0 %convolution_bitcast_fusion = f32[1024,128]{0,1:T(8,128)} fusion(bf16[1024,1024]{1,0:T(8,128)(2,1)S(1)} %copy-done, bf16[2048,1024]{1,0:T(8,128)(2,1)} %fusion.3, bf16[2048,128]{1,0:T(8,128)(2,1)S(1)} %copy-done.5, f32[128]{0:T(128)S(1)} %add_sqrt_fusion.1, f32[128]{0:T(128)S(1)} %broadcast_multiply_fusion.1), kind=kOutput, calls=%fused_computation.25 | convolution fusion | flops 806486016 | bytes 7341056 | tf_op jit(solution)/shard_map/dot_general | solution.py:71
  13.6 1.2 copy.34
  15.1 4.6 %divide_convert_fusion = bf16[1024,4,128]{2,1,0:T(4,128)(2,1)} fusion(f32[1024,4]{1,0:T(8,128)S(1)} %broadcast_add_fusion, f32[1024,128]{1,0:T(8,128)S(1)} %copy.34), kind=kLoop, calls=%fused_computation.16 | loop fusion | flops 1048576 | bytes 1589248 | tf_op jit(solution)/shard_map/convert_element_type | solution.py:74
  19.7 7.3 %convolution_convert_fusion = bf16[512,2048]{1,0:T(8,128)(2,1)} fusion(bf16[2048,1024]{1,0:T(8,128)(2,1)} %fusion.3, bf16[1024,1024]{1,0:T(8,128)(2,1)S(1)} %copy-done, bf16[128,8,4,128]{3,2,1,0:T(4,128)(2,1)} %bitcast.288), kind=kOutput, calls=%fused_computation.15 | convolution fusion | flops 3222798336 | bytes 9437184 | tf_op jit(solution)/shard_map/dot_general | solution.py:81
  27.0 1.7 fusion.66
  28.7 1.6 fusion.65
  30.3 1.6 fusion.64
  31.8 1.6 fusion.63
  33.4 1.6 fusion.62
  34.9 1.6 fusion.61
  36.5 1.6 fusion.60
  38.1 1.6 fusion.59
  39.6 0.7 fusion.58
  40.3 0.7 fusion.57
  40.9 0.7 fusion.56
  41.6 0.7 fusion.55
  42.3 0.6 fusion.54
  42.9 0.7 fusion.53
  43.6 0.6 fusion.52
  44.2 0.7 fusion.51
  44.9 6.6 %all-to-all-start = ((bf16[16,4,8,1,2048]{4,2,1,3,0:T(8,128)(2,1)}), bf16[16,4,8,1,2048]{4,2,1,3,0:T(8,128)(2,1)}, u32[]{:S(2)}, u32[]{:S(2)}) async-start(bf16[16,4,8,1,2048]{4,2,1,3,0:T(8,128)(2,1)} %fusion.51), calls=%async_computation | async-start | bytes 4194304 | tf_op jit(solution)/shard_map/all_to_all | solution.py:15
  51.9 47.1 %all-to-all-done = bf16[16,4,8,1,2048]{4,2,1,3,0:T(8,128)(2,1)} async-done(((bf16[16,4,8,1,2048]{4,2,1,3,0:T(8,128)(2,1)}), bf16[16,4,8,1,2048]{4,2,1,3,0:T(8,128)(2,1)}, u32[]{:S(2)}, u32[]{:S(2)}) %all-to-all-start) | async-done | bytes 2097184 | tf_op jit(solution)/shard_map/all_to_all | solution.py:15
  99.0 2.7 copy.35
  101.7 0.4 fusion.92
  102.1 0.9 copy-done.2
  103.0 0.7 fusion.18
  104.0 46.9 %custom-call.15 = f32[8,64,64]{2,1,0:T(8,128)S(1)} custom-call(f32[8,64,64]{2,1,0:T(8,128)S(1)} %fusion.50), custom_call_target="Cholesky" | custom-call | tf_op jit(solution)/shard_map/jit(cholesky)/cholesky | solution.py:47
  151.2 39.3 %custom-call.17 = f32[8,1,64,64]{2,3,1,0:T(8,128)S(1)} custom-call(f32[8,1,64,64]{3,2,1,0:T(8,128)S(1)} %select_bitcast_fusion.2), custom_call_target="InvertDiagBlocksLowerTriangular" | custom-call | tf_op jit(solution)/shard_map/triangular_solve/custom-call.2 | solution.py:51
  190.5 2.4 convolution_bitcast_fusion.4
  193.2 0.5 fusion.48
  193.8 0.4 fusion.90
  194.2 0.8 fusion.21
  195.2 46.9 %custom-call.18 = f32[8,64,64]{2,1,0:T(8,128)S(1)} custom-call(f32[8,64,64]{2,1,0:T(8,128)S(1)} %fusion.46), custom_call_target="Cholesky" | custom-call | tf_op jit(solution)/shard_map/jit(cholesky)/cholesky | solution.py:47
  242.3 39.3 %custom-call.20 = f32[8,1,64,64]{2,3,1,0:T(8,128)S(1)} custom-call(f32[8,1,64,64]{3,2,1,0:T(8,128)S(1)} %select_bitcast_fusion.1), custom_call_target="InvertDiagBlocksLowerTriangular" | custom-call | tf_op jit(solution)/shard_map/triangular_solve/custom-call.2 | solution.py:51
  281.7 2.4 fusion.81
  284.1 0.4 convolution_bitcast_fusion.2
  284.4 0.5 fusion.44
  285.0 0.4 fusion.88
  285.4 0.7 fusion.24
  286.3 47.1 %custom-call.21 = f32[8,64,64]{2,1,0:T(8,128)S(1)} custom-call(f32[8,64,64]{2,1,0:T(8,128)S(1)} %fusion.42), custom_call_target="Cholesky" | custom-call | tf_op jit(solution)/shard_map/jit(cholesky)/cholesky | solution.py:47
  333.7 39.3 %custom-call.23 = f32[8,1,64,64]{2,3,1,0:T(8,128)S(1)} custom-call(f32[8,1,64,64]{3,2,1,0:T(8,128)S(1)} %select_bitcast_fusion), custom_call_target="InvertDiagBlocksLowerTriangular" | custom-call | tf_op jit(solution)/shard_map/triangular_solve/custom-call.2 | solution.py:51
  373.0 2.2 fusion.79
  375.6 0.5 fusion.40
  376.2 0.6 add_bitcast_fusion
  (52 shorter events, 3.4 us)
Async XLA Ops:
  0.0 8.6 %copy-start = (bf16[1024,1024]{1,0:T(8,128)(2,1)S(1)}, bf16[1024,1024]{1,0:T(8,128)(2,1)}, u32[]{:S(2)}) copy-start(bf16[1024,1024]{1,0:T(8,128)(2,1)} %param.11) | copy-start | bytes 6291460
  0.0 3.6 copy-start.1
  4.8 3.2 copy-start.5
  8.6 6.3 %copy-start.7 = (f32[1,1024]{1,0:T(1,128)S(1)}, f32[1,1024]{1,0:T(1,128)}, u32[]{:S(2)}) copy-start(f32[1,1024]{1,0:T(1,128)} %param.12) | copy-start | bytes 12292
  8.6 6.3 %copy-start.8 = (f32[4]{0:T(128)S(1)}, f32[4]{0:T(128)}, u32[]{:S(2)}) copy-start(f32[4]{0:T(128)} %constant.65.clone) | copy-start | bytes 52
  27.0 12.6 %copy-start.6 = (bf16[512,2048]{1,0:T(8,128)(2,1)S(1)}, bf16[512,2048]{1,0:T(8,128)(2,1)}, u32[]{:S(2)}) copy-start(bf16[512,2048]{1,0:T(8,128)(2,1)} %convolution_convert_fusion) | copy-start | bytes 6291460
  44.9 54.1 %all-to-all-start = ((bf16[16,4,8,1,2048]{4,2,1,3,0:T(8,128)(2,1)}), bf16[16,4,8,1,2048]{4,2,1,3,0:T(8,128)(2,1)}, u32[]{:S(2)}, u32[]{:S(2)}) async-start(bf16[16,4,8,1,2048]{4,2,1,3,0:T(8,128)(2,1)} %fusion.51), calls=%async_computation | async-start | bytes 4194304 | tf_op jit(solution)/shard_map/all_to_all | solution.py:15
  101.7 1.4 copy-start.2
  190.5 3.3 copy-start.3
  281.7 3.3 copy-start.4
